TPU v7x, 32 devices: a whole 2x2x4 slice. The times are simulated.
32 devices in a mesh: visit: 2 (over x), patch: 16 (over z, y, core).
Axes of the slice: x: 2, y: 2, z: 4, core: 2. Of those that a mesh axis runs over, the one named last changes fastest.
Arguments:
- images: bfloat16 [2, 96, 128, 512], P('visit', 'patch'), may hold values from -12 to 12
- coefficients: float32 [2, 96, 3, 40], P('visit', 'patch'), may hold values from -2 to 2
- intersection: int32 [2, 96, 2], P('visit'), may hold values from 0 to 15, as said below
- row_offset: int32 [2, 96], P('visit'), may hold values from 0 to 7
- col_offset: int32 [2, 96], P('visit'), may hold values from 0 to 511
- shifts: float32 [2, 96, 2], P('visit'), may hold values from 0 to 1
- inv_var: float32 [2, 96], P('visit'), may hold values from 0.3 to 3
Outputs:
- coadd: float32 [128, 8192], P('visit', 'patch')
- detection: float32 [128, 8192], P('visit', 'patch')
Inputs may be any that keep to these rules, and one draw needn't show every extreme that they name: intersection[v, c, 1] = intersection[v, c, 0] + 1. Within each aligned block of 6 exposures of a visit (c from b * 6 to (b + 1) * 6 - 1), no patch is named twice.
All inputs are finite; a program needn't handle non-finite values.
Results may differ from a plain program's by a relative error of at most 0.0061.
Values may be sent and summed in bfloat16 or wider, within the bound.
No kernel may reach another device: no remote copies, remote signals or barrier semaphores. Data moves between devices by JAX's collectives and lax.ppermute only.
A program may use at most 128 MiB of HBM per device.

v0:
```python
import jax
import jax.numpy as jnp
from jax import lax
from jax.sharding import PartitionSpec as P

KRAD = 10
DRAD = 4
WIDTHS_PX = (1.0, 1.7, 2.6, 3.6)


def extended(array, sides, width):
    for axis, dim in sides:
        peers, length = (lax.axis_size(axis), array.shape[dim])
        up = [(i, (i + 1) % peers) for i in range(peers - 1)]
        down = [(j, i) for i, j in up]
        last = lax.slice_in_dim(array, length - width, length, axis=dim)
        initial = lax.slice_in_dim(array, 0, width, axis=dim)
        before = lax.ppermute(last, axis, up)
        after = lax.ppermute(initial, axis, down)
        array = jnp.concatenate([before, array, after], axis=dim)
    return array


def kernel_value(offsets, width_px, degree):
    scaled = offsets / width_px
    return scaled**degree * jnp.exp(-offsets * offsets / (2.0 * width_px * width_px))


def band_tables(radius, extent):
    offsets = jnp.arange(-radius, radius + 1).astype(jnp.float32)
    distance = (jnp.arange(extent)[None, :] - jnp.arange(extent)[:, None]).astype(jnp.float32)
    inside = jnp.abs(distance) <= radius
    tables = []
    for group in range(4):
        for degree in range(4):
            profile = kernel_value(offsets, WIDTHS_PX[group], degree)
            norm_value = jnp.sqrt(jnp.sum(profile * profile))
            values = kernel_value(distance, WIDTHS_PX[group], degree) / norm_value
            tables.append(jnp.where(inside, values, 0.0).astype(jnp.bfloat16))
    return jnp.stack(tables).reshape(4, 4, extent, extent)


def match_exposure(exposure, weights, row_band, col_band, row_pos, col_pos):
    smoothed = jnp.einsum(
        "gdri,iw->gdrw", row_band, exposure, preferred_element_type=jnp.float32
    ).astype(jnp.bfloat16)
    matched = jnp.zeros(exposure.shape, jnp.float32)
    term = 0
    for group in range(4):
        for x_degree in range(4):
            count = 4 - x_degree
            response = jnp.einsum(
                "drw,xw->drx",
                smoothed[group, :count],
                col_band[group, x_degree],
                preferred_element_type=jnp.float32,
            )
            picked = weights[:, term : term + count]
            steady = jnp.sum(picked[0][:, None, None] * response, 0)
            along_rows = jnp.sum(picked[1][:, None, None] * response, 0)
            along_cols = jnp.sum(picked[2][:, None, None] * response, 0)
            matched = (
                matched + steady + row_pos[:, None] * along_rows + col_pos[None, :] * along_cols
            )
            term += count
    return matched.astype(jnp.bfloat16)


def warp_exposure(exposure, row_shift, col_shift, frac_row, frac_col, weight):
    row_count, col_count = exposure.shape
    nothing = jnp.zeros((), jnp.bfloat16)
    upper = (1.0 - frac_row).astype(jnp.bfloat16)
    lower = frac_row.astype(jnp.bfloat16)
    left = (1.0 - frac_col).astype(jnp.bfloat16)
    right = frac_col.astype(jnp.bfloat16)
    target_row = jnp.arange(row_count)[:, None]
    source_row = jnp.arange(row_count)[None, :]
    row_map = jnp.where(source_row == target_row - row_shift, upper, nothing) + jnp.where(
        source_row == target_row - row_shift - 1, lower, nothing
    )
    source_col = jnp.arange(col_count)[:, None]
    target_col = jnp.arange(col_count)[None, :]
    col_map = jnp.where(source_col == target_col - col_shift, left, nothing) + jnp.where(
        source_col == target_col - col_shift - 1, right, nothing
    )
    middle = jnp.dot(row_map, exposure, preferred_element_type=jnp.float32).astype(jnp.bfloat16)
    warped = jnp.dot(middle, col_map, preferred_element_type=jnp.float32)
    row_cover = jnp.sum(row_map.astype(jnp.float32), 1)
    col_cover = jnp.sum(col_map.astype(jnp.float32), 0)
    return (weight * warped, weight * row_cover[:, None] * col_cover[None, :])


def detect(framed, radius):
    offsets = jnp.arange(-radius, radius + 1).astype(jnp.float32)
    profile = jnp.exp(-offsets * offsets / 8.0)
    profile = profile / jnp.sqrt(jnp.sum(profile * profile))
    row_count = framed.shape[0] - 2 * radius
    col_count = framed.shape[1] - 2 * radius
    across = jnp.zeros((row_count, framed.shape[1]), jnp.float32)
    for tap_idx in range(2 * radius + 1):
        across = across + profile[tap_idx] * framed[tap_idx : tap_idx + row_count]
    result = jnp.zeros((row_count, col_count), jnp.float32)
    for tap_idx in range(2 * radius + 1):
        result = result + profile[tap_idx] * across[:, tap_idx : tap_idx + col_count]
    return result


def local(images, coefficients, intersection, row_offset, col_offset, shifts, inv_var):
    exposures = images[0]
    weights_all = coefficients[0]
    row_count = exposures.shape[1]
    col_count = exposures.shape[2]
    table = intersection[0]
    row_shifts = row_offset[0]
    col_shifts = col_offset[0]
    fractions = shifts[0]
    inverse = inv_var[0]
    own_patch = lax.axis_index("patch")
    row_band = band_tables(KRAD, row_count)
    col_band = band_tables(KRAD, col_count)
    row_pos = (2.0 * jnp.arange(row_count).astype(jnp.float32) + 1.0) / row_count - 1.0
    col_pos = (2.0 * jnp.arange(col_count).astype(jnp.float32) + 1.0) / col_count - 1.0
    matched = lax.map(
        lambda operands: match_exposure(
            operands[0], operands[1], row_band, col_band, row_pos, col_pos
        ),
        (exposures, weights_all),
    )
    empty = (
        jnp.zeros((row_count, col_count), jnp.float32),
        jnp.zeros((row_count, col_count), jnp.float32),
    )

    def add_exposure(totals, exposure, ccd, hit_first):
        col_shift = jnp.where(hit_first, col_shifts[ccd], col_shifts[ccd] - col_count)
        flux_part, cover_part = warp_exposure(
            exposure, row_shifts[ccd], col_shift, fractions[ccd, 0], fractions[ccd, 1], inverse[ccd]
        )
        return (totals[0] + flux_part, totals[1] + cover_part)

    arrived = lax.all_gather(matched, "patch", axis=0, tiled=True)

    def visit_one(offset, inner):
        hit_first = table[offset, 0] == own_patch
        hit_second = table[offset, 1] == own_patch
        exposure = lax.dynamic_index_in_dim(arrived, offset, 0, keepdims=False)
        return lax.cond(
            hit_first | hit_second,
            lambda: add_exposure(inner, exposure, offset, hit_first),
            lambda: inner,
        )

    flux_sum, cover_sum = lax.fori_loop(0, arrived.shape[0], visit_one, empty)
    flux_part, cover_part = (
        lax.psum_scatter(flux_sum, "visit", scatter_dimension=0, tiled=True),
        lax.psum_scatter(cover_sum, "visit", scatter_dimension=0, tiled=True),
    )
    coadd = flux_part / jnp.maximum(cover_part, 1.0)
    framed = extended(coadd, (("visit", 0), ("patch", 1)), DRAD)
    detection = detect(framed, DRAD)
    return (coadd, detection)


def solution(mesh):
    return jax.shard_map(
        local,
        mesh=mesh,
        in_specs=(
            P("visit", "patch", None, None),
            P("visit", "patch", None, None),
            P("visit", None, None),
            P("visit", None),
            P("visit", None),
            P("visit", None, None),
            P("visit", None),
        ),
        out_specs=(P("visit", "patch"), P("visit", "patch")),
        check_vma=False,
    )
```

profile of v0, /device:TPU:5, one launch (start us, length us, event | category | flops | bytes accessed | tf_op | source)
XLA Modules:
  0.0 671.8 jit_solution(11030103022260496552)
XLA Ops:
  32.3 1.4 fusion.115
  38.0 1.4 fusion.112
  43.7 1.4 fusion.113
  49.4 1.4 fusion.114
  51.3 119.2 %while.28 = (s32[]{:T(128)}, bf16[6,128,512]{2,1,0:T(8,128)(2,1)S(1)}, f32[6,3,40]{2,1,0:T(4,128)S(1)}, bf16[6,128,512]{1,2,0:T(8,128)(2,1)S(1)}, bf16[4,4,128,1...) while((s32[]{:T(128)}, ...), condition=%wide.region_53.54_spmd.clone.clone, body=%wide.region_16.53_spmd.clone.clone.sunk | while | flops 2971667456 | bytes 70542368 | solution.py:123
  52.3 2.0 multiply_reduce_fusion.58
  54.4 1.7 multiply_reduce_fusion.59
  62.8 8.5 %fusion.219 = bf16[6,128,512]{2,1,0:T(8,128)(2,1)S(1)} fusion(bf16[6,128,512]{2,1,0:T(8,128)(2,1)S(1)} %get-tuple-element.857, s32[]{:T(128)} %get-tuple-element.856, bf16[4,4,512,512]{3,2,1,0:T(8,128)(2,1)S(1)} %copy-done, f32[128,512]{1,0:T(8,128)S(1)} %get-tuple-element.764, f32[128,512]{1,0:T(8,128)S(1)} %get-tuple-element.765, ...), kind=kOutput, calls=%fused_computation.133.clone.1 | convolution fusion | flops 73138176 | bytes 11012660 | tf_op jit(solution)/shard_map/while/body/eval_jaxpr/drw,xw->drx/dot_general | solution.py:52
  72.2 2.0 multiply_reduce_fusion.58
  74.2 1.7 multiply_reduce_fusion.59
  82.6 8.5 %fusion.219 = bf16[6,128,512]{2,1,0:T(8,128)(2,1)S(1)} fusion(bf16[6,128,512]{2,1,0:T(8,128)(2,1)S(1)} %get-tuple-element.857, s32[]{:T(128)} %get-tuple-element.856, bf16[4,4,512,512]{3,2,1,0:T(8,128)(2,1)S(1)} %copy-done, f32[128,512]{1,0:T(8,128)S(1)} %get-tuple-element.764, f32[128,512]{1,0:T(8,128)S(1)} %get-tuple-element.765, ...), kind=kOutput, calls=%fused_computation.133.clone.1 | convolution fusion | flops 73138176 | bytes 11012660 | tf_op jit(solution)/shard_map/while/body/eval_jaxpr/drw,xw->drx/dot_general | solution.py:52
  92.0 2.0 multiply_reduce_fusion.58
  94.1 1.7 multiply_reduce_fusion.59
  102.4 8.5 %fusion.219 = bf16[6,128,512]{2,1,0:T(8,128)(2,1)S(1)} fusion(bf16[6,128,512]{2,1,0:T(8,128)(2,1)S(1)} %get-tuple-element.857, s32[]{:T(128)} %get-tuple-element.856, bf16[4,4,512,512]{3,2,1,0:T(8,128)(2,1)S(1)} %copy-done, f32[128,512]{1,0:T(8,128)S(1)} %get-tuple-element.764, f32[128,512]{1,0:T(8,128)S(1)} %get-tuple-element.765, ...), kind=kOutput, calls=%fused_computation.133.clone.1 | convolution fusion | flops 73138176 | bytes 11012660 | tf_op jit(solution)/shard_map/while/body/eval_jaxpr/drw,xw->drx/dot_general | solution.py:52
  111.8 2.0 multiply_reduce_fusion.58
  113.9 1.7 multiply_reduce_fusion.59
  122.3 8.5 %fusion.219 = bf16[6,128,512]{2,1,0:T(8,128)(2,1)S(1)} fusion(bf16[6,128,512]{2,1,0:T(8,128)(2,1)S(1)} %get-tuple-element.857, s32[]{:T(128)} %get-tuple-element.856, bf16[4,4,512,512]{3,2,1,0:T(8,128)(2,1)S(1)} %copy-done, f32[128,512]{1,0:T(8,128)S(1)} %get-tuple-element.764, f32[128,512]{1,0:T(8,128)S(1)} %get-tuple-element.765, ...), kind=kOutput, calls=%fused_computation.133.clone.1 | convolution fusion | flops 73138176 | bytes 11012660 | tf_op jit(solution)/shard_map/while/body/eval_jaxpr/drw,xw->drx/dot_general | solution.py:52
  131.7 2.0 multiply_reduce_fusion.58
  133.7 1.7 multiply_reduce_fusion.59
  142.1 8.5 %fusion.219 = bf16[6,128,512]{2,1,0:T(8,128)(2,1)S(1)} fusion(bf16[6,128,512]{2,1,0:T(8,128)(2,1)S(1)} %get-tuple-element.857, s32[]{:T(128)} %get-tuple-element.856, bf16[4,4,512,512]{3,2,1,0:T(8,128)(2,1)S(1)} %copy-done, f32[128,512]{1,0:T(8,128)S(1)} %get-tuple-element.764, f32[128,512]{1,0:T(8,128)S(1)} %get-tuple-element.765, ...), kind=kOutput, calls=%fused_computation.133.clone.1 | convolution fusion | flops 73138176 | bytes 11012660 | tf_op jit(solution)/shard_map/while/body/eval_jaxpr/drw,xw->drx/dot_general | solution.py:52
  151.5 2.0 multiply_reduce_fusion.58
  153.6 1.7 multiply_reduce_fusion.59
  161.9 8.5 %fusion.219 = bf16[6,128,512]{2,1,0:T(8,128)(2,1)S(1)} fusion(bf16[6,128,512]{2,1,0:T(8,128)(2,1)S(1)} %get-tuple-element.857, s32[]{:T(128)} %get-tuple-element.856, bf16[4,4,512,512]{3,2,1,0:T(8,128)(2,1)S(1)} %copy-done, f32[128,512]{1,0:T(8,128)S(1)} %get-tuple-element.764, f32[128,512]{1,0:T(8,128)S(1)} %get-tuple-element.765, ...), kind=kOutput, calls=%fused_computation.133.clone.1 | convolution fusion | flops 73138176 | bytes 11012660 | tf_op jit(solution)/shard_map/while/body/eval_jaxpr/drw,xw->drx/dot_general | solution.py:52
  171.5 101.2 %all-gather.2.cloned.1.call-done = bf16[96,128,512]{2,1,0:T(8,128)(2,1)} async-done(((bf16[6,128,512]{2,1,0:T(8,128)(2,1)}), bf16[96,128,512]{2,1,0:T(8,128)(2,1)}) %all-gather.2.cloned.1.call-update) | async-done | bytes 12582928 | tf_op jit(solution)/shard_map/all_gather | solution.py:141
  272.8 335.8 %while.27 = (s32[]{:T(128)}, f32[128,512]{1,0:T(8,128)S(1)}, f32[128,512]{1,0:T(8,128)S(1)}, s32[96,2]{0,1:T(2,128)S(1)}, s32[]{:T(128)}, /*index=5*/f32[96]{0:T...) while((s32[]{:T(128)}, f32[128,512]{1,0:T(8,128)S(1)}, ...), condition=%wide.region_59.60_spmd, body=%wide.region_54.59_spmd.sunk | while | flops 88949520 | bytes 1204658 | solution.py:153
  282.8 9.6 %conditional.2 = ((f32[128,512]{1,0:T(8,128)S(1)}, f32[128,512]{1,0:T(8,128)S(1)})) conditional(s32[]{:T(128)} %convert_element_type.1283, (f32[128,512]{1,0:T(8,128)S(1)}, f32[128,512]{1,0:T(8,128)S(1)}) %tuple.161, (s32[]{:T(128)}, f32[96]{0:T(128)S(1)}, s32[96]{0:T(128)S(1)}, f32[96,2]{0,1:T(2,128)S(1)}, bf16[96,128,512]{2,1,0:T(8,128)(2,1)}, ...), branch_computations={%region_55.55_spmd, %region_56.58_spmd} | conditional | flops 88949512 | bytes 1204415 | solution.py:147
  290.5 1.9 fusion.4
  318.3 9.6 %conditional.2 = ((f32[128,512]{1,0:T(8,128)S(1)}, f32[128,512]{1,0:T(8,128)S(1)})) conditional(s32[]{:T(128)} %convert_element_type.1283, (f32[128,512]{1,0:T(8,128)S(1)}, f32[128,512]{1,0:T(8,128)S(1)}) %tuple.161, (s32[]{:T(128)}, f32[96]{0:T(128)S(1)}, s32[96]{0:T(128)S(1)}, f32[96,2]{0,1:T(2,128)S(1)}, bf16[96,128,512]{2,1,0:T(8,128)(2,1)}, ...), branch_computations={%region_55.55_spmd, %region_56.58_spmd} | conditional | flops 88949512 | bytes 1204415 | solution.py:147
  326.0 1.9 fusion.4
  337.9 9.6 %conditional.2 = ((f32[128,512]{1,0:T(8,128)S(1)}, f32[128,512]{1,0:T(8,128)S(1)})) conditional(s32[]{:T(128)} %convert_element_type.1283, (f32[128,512]{1,0:T(8,128)S(1)}, f32[128,512]{1,0:T(8,128)S(1)}) %tuple.161, (s32[]{:T(128)}, f32[96]{0:T(128)S(1)}, s32[96]{0:T(128)S(1)}, f32[96,2]{0,1:T(2,128)S(1)}, bf16[96,128,512]{2,1,0:T(8,128)(2,1)}, ...), branch_computations={%region_55.55_spmd, %region_56.58_spmd} | conditional | flops 88949512 | bytes 1204415 | solution.py:147
  345.6 1.9 fusion.4
  357.5 9.6 %conditional.2 = ((f32[128,512]{1,0:T(8,128)S(1)}, f32[128,512]{1,0:T(8,128)S(1)})) conditional(s32[]{:T(128)} %convert_element_type.1283, (f32[128,512]{1,0:T(8,128)S(1)}, f32[128,512]{1,0:T(8,128)S(1)}) %tuple.161, (s32[]{:T(128)}, f32[96]{0:T(128)S(1)}, s32[96]{0:T(128)S(1)}, f32[96,2]{0,1:T(2,128)S(1)}, bf16[96,128,512]{2,1,0:T(8,128)(2,1)}, ...), branch_computations={%region_55.55_spmd, %region_56.58_spmd} | conditional | flops 88949512 | bytes 1204415 | solution.py:147
  365.2 1.9 fusion.4
  377.1 9.6 %conditional.2 = ((f32[128,512]{1,0:T(8,128)S(1)}, f32[128,512]{1,0:T(8,128)S(1)})) conditional(s32[]{:T(128)} %convert_element_type.1283, (f32[128,512]{1,0:T(8,128)S(1)}, f32[128,512]{1,0:T(8,128)S(1)}) %tuple.161, (s32[]{:T(128)}, f32[96]{0:T(128)S(1)}, s32[96]{0:T(128)S(1)}, f32[96,2]{0,1:T(2,128)S(1)}, bf16[96,128,512]{2,1,0:T(8,128)(2,1)}, ...), branch_computations={%region_55.55_spmd, %region_56.58_spmd} | conditional | flops 88949512 | bytes 1204415 | solution.py:147
  384.8 1.9 fusion.4
  394.7 9.6 %conditional.2 = ((f32[128,512]{1,0:T(8,128)S(1)}, f32[128,512]{1,0:T(8,128)S(1)})) conditional(s32[]{:T(128)} %convert_element_type.1283, (f32[128,512]{1,0:T(8,128)S(1)}, f32[128,512]{1,0:T(8,128)S(1)}) %tuple.161, (s32[]{:T(128)}, f32[96]{0:T(128)S(1)}, s32[96]{0:T(128)S(1)}, f32[96,2]{0,1:T(2,128)S(1)}, bf16[96,128,512]{2,1,0:T(8,128)(2,1)}, ...), branch_computations={%region_55.55_spmd, %region_56.58_spmd} | conditional | flops 88949512 | bytes 1204415 | solution.py:147
  402.4 1.9 fusion.4
  416.3 9.6 %conditional.2 = ((f32[128,512]{1,0:T(8,128)S(1)}, f32[128,512]{1,0:T(8,128)S(1)})) conditional(s32[]{:T(128)} %convert_element_type.1283, (f32[128,512]{1,0:T(8,128)S(1)}, f32[128,512]{1,0:T(8,128)S(1)}) %tuple.161, (s32[]{:T(128)}, f32[96]{0:T(128)S(1)}, s32[96]{0:T(128)S(1)}, f32[96,2]{0,1:T(2,128)S(1)}, bf16[96,128,512]{2,1,0:T(8,128)(2,1)}, ...), branch_computations={%region_55.55_spmd, %region_56.58_spmd} | conditional | flops 88949512 | bytes 1204415 | solution.py:147
  424.0 1.9 fusion.4
  437.9 9.6 %conditional.2 = ((f32[128,512]{1,0:T(8,128)S(1)}, f32[128,512]{1,0:T(8,128)S(1)})) conditional(s32[]{:T(128)} %convert_element_type.1283, (f32[128,512]{1,0:T(8,128)S(1)}, f32[128,512]{1,0:T(8,128)S(1)}) %tuple.161, (s32[]{:T(128)}, f32[96]{0:T(128)S(1)}, s32[96]{0:T(128)S(1)}, f32[96,2]{0,1:T(2,128)S(1)}, bf16[96,128,512]{2,1,0:T(8,128)(2,1)}, ...), branch_computations={%region_55.55_spmd, %region_56.58_spmd} | conditional | flops 88949512 | bytes 1204415 | solution.py:147
  445.6 1.9 fusion.4
  465.4 9.6 %conditional.2 = ((f32[128,512]{1,0:T(8,128)S(1)}, f32[128,512]{1,0:T(8,128)S(1)})) conditional(s32[]{:T(128)} %convert_element_type.1283, (f32[128,512]{1,0:T(8,128)S(1)}, f32[128,512]{1,0:T(8,128)S(1)}) %tuple.161, (s32[]{:T(128)}, f32[96]{0:T(128)S(1)}, s32[96]{0:T(128)S(1)}, f32[96,2]{0,1:T(2,128)S(1)}, bf16[96,128,512]{2,1,0:T(8,128)(2,1)}, ...), branch_computations={%region_55.55_spmd, %region_56.58_spmd} | conditional | flops 88949512 | bytes 1204415 | solution.py:147
  473.2 1.9 fusion.4
  487.0 9.6 %conditional.2 = ((f32[128,512]{1,0:T(8,128)S(1)}, f32[128,512]{1,0:T(8,128)S(1)})) conditional(s32[]{:T(128)} %convert_element_type.1283, (f32[128,512]{1,0:T(8,128)S(1)}, f32[128,512]{1,0:T(8,128)S(1)}) %tuple.161, (s32[]{:T(128)}, f32[96]{0:T(128)S(1)}, s32[96]{0:T(128)S(1)}, f32[96,2]{0,1:T(2,128)S(1)}, bf16[96,128,512]{2,1,0:T(8,128)(2,1)}, ...), branch_computations={%region_55.55_spmd, %region_56.58_spmd} | conditional | flops 88949512 | bytes 1204415 | solution.py:147
  494.7 1.9 fusion.4
  512.6 9.6 %conditional.2 = ((f32[128,512]{1,0:T(8,128)S(1)}, f32[128,512]{1,0:T(8,128)S(1)})) conditional(s32[]{:T(128)} %convert_element_type.1283, (f32[128,512]{1,0:T(8,128)S(1)}, f32[128,512]{1,0:T(8,128)S(1)}) %tuple.161, (s32[]{:T(128)}, f32[96]{0:T(128)S(1)}, s32[96]{0:T(128)S(1)}, f32[96,2]{0,1:T(2,128)S(1)}, bf16[96,128,512]{2,1,0:T(8,128)(2,1)}, ...), branch_computations={%region_55.55_spmd, %region_56.58_spmd} | conditional | flops 88949512 | bytes 1204415 | solution.py:147
  520.3 1.9 fusion.4
  528.2 9.6 %conditional.2 = ((f32[128,512]{1,0:T(8,128)S(1)}, f32[128,512]{1,0:T(8,128)S(1)})) conditional(s32[]{:T(128)} %convert_element_type.1283, (f32[128,512]{1,0:T(8,128)S(1)}, f32[128,512]{1,0:T(8,128)S(1)}) %tuple.161, (s32[]{:T(128)}, f32[96]{0:T(128)S(1)}, s32[96]{0:T(128)S(1)}, f32[96,2]{0,1:T(2,128)S(1)}, bf16[96,128,512]{2,1,0:T(8,128)(2,1)}, ...), branch_computations={%region_55.55_spmd, %region_56.58_spmd} | conditional | flops 88949512 | bytes 1204415 | solution.py:147
  535.9 1.9 fusion.4
  553.8 9.6 %conditional.2 = ((f32[128,512]{1,0:T(8,128)S(1)}, f32[128,512]{1,0:T(8,128)S(1)})) conditional(s32[]{:T(128)} %convert_element_type.1283, (f32[128,512]{1,0:T(8,128)S(1)}, f32[128,512]{1,0:T(8,128)S(1)}) %tuple.161, (s32[]{:T(128)}, f32[96]{0:T(128)S(1)}, s32[96]{0:T(128)S(1)}, f32[96,2]{0,1:T(2,128)S(1)}, bf16[96,128,512]{2,1,0:T(8,128)(2,1)}, ...), branch_computations={%region_55.55_spmd, %region_56.58_spmd} | conditional | flops 88949512 | bytes 1204415 | solution.py:147
  561.5 1.9 fusion.4
  569.4 9.6 %conditional.2 = ((f32[128,512]{1,0:T(8,128)S(1)}, f32[128,512]{1,0:T(8,128)S(1)})) conditional(s32[]{:T(128)} %convert_element_type.1283, (f32[128,512]{1,0:T(8,128)S(1)}, f32[128,512]{1,0:T(8,128)S(1)}) %tuple.161, (s32[]{:T(128)}, f32[96]{0:T(128)S(1)}, s32[96]{0:T(128)S(1)}, f32[96,2]{0,1:T(2,128)S(1)}, bf16[96,128,512]{2,1,0:T(8,128)(2,1)}, ...), branch_computations={%region_55.55_spmd, %region_56.58_spmd} | conditional | flops 88949512 | bytes 1204415 | solution.py:147
  577.1 1.9 fusion.4
  595.0 9.6 %conditional.2 = ((f32[128,512]{1,0:T(8,128)S(1)}, f32[128,512]{1,0:T(8,128)S(1)})) conditional(s32[]{:T(128)} %convert_element_type.1283, (f32[128,512]{1,0:T(8,128)S(1)}, f32[128,512]{1,0:T(8,128)S(1)}) %tuple.161, (s32[]{:T(128)}, f32[96]{0:T(128)S(1)}, s32[96]{0:T(128)S(1)}, f32[96,2]{0,1:T(2,128)S(1)}, bf16[96,128,512]{2,1,0:T(8,128)(2,1)}, ...), branch_computations={%region_55.55_spmd, %region_56.58_spmd} | conditional | flops 88949512 | bytes 1204415 | solution.py:147
  602.7 1.9 fusion.4
  611.4 8.4 %reduce-scatter.3.cloned.1.call-done = f32[64,512]{1,0:T(8,128)} async-done(((f32[128,512]{1,0:T(8,128)}), f32[64,512]{1,0:T(8,128)}) %reduce-scatter.3.cloned.1.call-update) | async-done | bytes 131088 | tf_op jit(solution)/shard_map/reduce_scatter | solution.py:155
  619.7 14.0 %reduce-scatter.5.cloned.1.call-done = f32[64,512]{1,0:T(8,128)} async-done(((f32[128,512]{1,0:T(8,128)}), f32[64,512]{1,0:T(8,128)}) %reduce-scatter.5.cloned.1.call-update) | async-done | bytes 131088 | tf_op jit(solution)/shard_map/reduce_scatter | solution.py:156
  634.8 2.2 collective-permute-start
  638.3 3.1 collective-permute-done.1
  641.4 5.3 collective-permute-start.2
  646.7 1.9 collective-permute-start.3
  649.3 3.6 collective-permute-done.3
  653.0 5.7 fusion.128
  658.7 6.5 fusion.136
  (552 shorter events, 202.2 us)
Async XLA Ops:
  7.2 43.7 %copy-start.4 = (bf16[1,6,128,512]{3,2,1,0:T(8,128)(2,1)S(1)}, bf16[1,6,128,512]{3,2,1,0:T(8,128)(2,1)}, u32[]{:S(2)}) copy-start(bf16[1,6,128,512]{3,2,1,0:T(8,128)(2,1)} %param.13) | copy-start | bytes 2359300
  7.2 44.1 %copy-start.8 = (f32[1,6,3,40]{3,0,2,1:T(1,128)S(1)}, f32[1,6,3,40]{3,0,2,1:T(1,128)}, u32[]{:S(2)}) copy-start(f32[1,6,3,40]{3,0,2,1:T(1,128)} %param.14) | copy-start | bytes 8644
  7.2 265.5 %all-gather.2.cloned.1.call-start = ((), (), s32[]{:S(2)}) async-start(), calls=%async_computation.2 | async-start | bytes 13369344 | tf_op jit(solution)/shard_map/all_gather | solution.py:141
  51.3 221.5 %copy-start.6 = (s32[1,96,2]{1,2,0:T(2,128)S(1)}, s32[1,96,2]{1,2,0:T(2,128)}, u32[]{:S(2)}) copy-start(s32[1,96,2]{1,2,0:T(2,128)} %param.15) | copy-start | bytes 2308
  51.3 221.5 %copy-start.7 = (f32[1,96,2]{1,2,0:T(2,128)S(1)}, f32[1,96,2]{1,2,0:T(2,128)}, u32[]{:S(2)}) copy-start(f32[1,96,2]{1,2,0:T(2,128)} %param.18) | copy-start | bytes 2308
  51.3 221.5 %copy-start.9 = (f32[1,96]{1,0:T(1,128)S(1)}, f32[1,96]{1,0:T(1,128)}, u32[]{:S(2)}) copy-start(f32[1,96]{1,0:T(1,128)} %param.19) | copy-start | bytes 1156
  51.3 221.5 %copy-start.10 = (s32[1,96]{1,0:T(1,128)S(1)}, s32[1,96]{1,0:T(1,128)}, u32[]{:S(2)}) copy-start(s32[1,96]{1,0:T(1,128)} %param.16) | copy-start | bytes 1156
  51.3 221.5 %copy-start.11 = (s32[1,96]{1,0:T(1,128)S(1)}, s32[1,96]{1,0:T(1,128)}, u32[]{:S(2)}) copy-start(s32[1,96]{1,0:T(1,128)} %param.17) | copy-start | bytes 1156
  51.5 4.7 copy-start
  71.3 4.7 copy-start
  91.2 4.7 copy-start
  111.0 4.7 copy-start
  130.8 4.7 copy-start
  150.7 4.7 copy-start
  170.5 0.9 copy-start.5
  171.4 448.3 %reduce-scatter.3.cloned.1.call-start = ((), (), s32[]{:S(2)}) async-start(), calls=%async_computation.3 | async-start | bytes 393216 | tf_op jit(solution)/shard_map/reduce_scatter | solution.py:155
  608.6 0.7 copy-start.3
  608.6 0.8 copy-start.1
  609.3 24.4 %reduce-scatter.5.cloned.1.call-start = ((), (), s32[]{:S(2)}) async-start(), calls=%async_computation.4 | async-start | bytes 393216 | tf_op jit(solution)/shard_map/reduce_scatter | solution.py:156
  634.7 30.5 %copy-start.2 = (f32[64,512]{1,0:T(8,128)}, f32[64,512]{1,0:T(8,128)S(1)}, u32[]{:S(2)}) copy-start(f32[64,512]{1,0:T(8,128)S(1)} %maximum_divide_fusion) | copy-start | bytes 393220
  634.8 3.5 collective-permute-start
  636.9 4.4 collective-permute-start.1
  641.4 7.9 %collective-permute-start.2 = (f32[72,4]{1,0:T(8,128)S(1)}, f32[72,4]{1,0:T(8,128)S(1)}, u32[]{:S(2)}, u32[]{:S(2)}) collective-permute-start(f32[72,4]{1,0:T(8,128)S(1)} %get-tuple-element.558), channel_id=1, source_target_pairs={{0,1},{1,2},{2,3},{3,4},{4,5},{5,6},{6,7},{7,8},{8,9},{9,10},{10,1... | collective-permute-start | bytes 3464 | tf_op jit(solution)/shard_map/ppermute | solution.py:18
  646.7 6.2 collective-permute-start.3
Sparse Core Ops, SparseCore 0:
  171.6 101.1 all-gather.1
  609.4 10.2 reduce-scatter.2
  622.0 11.7 reduce-scatter.4
where the time goes:
time: 676 us; the launch traced here: 672 us
  loops' own time  185 us (27%)
  matrix products  141 us (21%)
  waiting for transfers between devices  131 us (19%)
  local copies, waits for them, and re-layouts  107 us (16%)
  other arithmetic  71.6 us (11%)
  between operations  25.4 us (4%)
  starting transfers between devices  10.8 us (2%)
    another operation x1, loops' own time, local(): flux_sum, cover_sum = lax.fori_loop(0, arrived.shape[0], visit_one, empty)  128 us
    dot_general x96, matrix products, match_exposure(): jnp.einsum('drw,xw->drx', smoothed[group, :count], col_band[group, x_degr...  108 us
    all_gather x1, waiting for transfers between devices, local(): arrived = lax.all_gather(matched, 'patch', axis=0, tiled=True)  101 us
    dynamic_slice x96, local copies, waits for them, and re-layouts, visit_one(): hit_second = table[offset, 1] == own_patch  62.7 us
    another operation x96, loops' own time, visit_one(): lax.cond(hit_first | hit_second, lambda: add_exposure(inner, exposure, of...  56 us
    dot_general x15, matrix products, warp_exposure(): warped = jnp.dot(middle, col_map, preferred_element_type=jnp.float32)  28.8 us
    unnamed x30, other arithmetic  21.1 us
    reduce_scatter x1, waiting for transfers between devices, local(): lax.psum_scatter(cover_sum, 'visit', scatter_dimension=0, tiled=True)  14 us
  transfers between devices with their start and end apart: 7, of which 5 were waited for; matrix products, arithmetic and copies ran while one was open for 0% of the time, Pallas kernels for 0%

commit v1 on v0

--- a/solution.py
+++ b/solution.py
@@ -6,6 +6,26 @@
 KRAD = 10
 DRAD = 4
 WIDTHS_PX = (1.0, 1.7, 2.6, 3.6)
+
+
+def divide_turns(sheet):
+    n_lanes = lax.axis_size("patch")
+    line_up = []
+    for b in range(n_lanes):
+        line_up.append((b, (b + 1) % n_lanes))
+    pieces_in = []
+    for b in range(n_lanes):
+        pieces_in.append((b, (b - 1) % n_lanes))
+    vec_out, odd = ([sheet], [sheet])
+    for _ in range(n_lanes // 2):
+        local_out = lax.ppermute(vec_out[-1], "patch", line_up)
+        vec_out.append(local_out)
+    for _ in range((n_lanes - 1) // 2):
+        a_now = lax.ppermute(odd[-1], "patch", pieces_in)
+        odd.append(a_now)
+    taken_in = jnp.concatenate([*vec_out[::-1], *odd[1:]], 0)
+    s_next = lax.axis_index("patch")
+    return jnp.roll(taken_in, (s_next - n_lanes // 2) * sheet.shape[0], 0)
 
 
 def extended(array, sides, width):
@@ -138,7 +158,7 @@
         )
         return (totals[0] + flux_part, totals[1] + cover_part)
 
-    arrived = lax.all_gather(matched, "patch", axis=0, tiled=True)
+    arrived = divide_turns(matched)
 
     def visit_one(offset, inner):
         hit_first = table[offset, 0] == own_patch

time: 676 us -> 744 us (1.10)
  starting transfers between devices: 10.8 us -> 101 us
  waiting for transfers between devices: 131 us -> 87 us
  local copies, waits for them, and re-layouts: 107 us -> 128 us
    all_gather x1 -> x0, waiting for transfers between devices: 101 us -> none  [local(): arrived = lax.all_gather(matched, 'patch', axis=0, tiled=True)]
    ppermute x0 -> x15, starting transfers between devices: none -> 90.3 us  [the longest x7 78.1 us: divide_turns(): a_now = lax.ppermute(odd[-1], 'patch', pieces_in)]
    ppermute x0 -> x15, waiting for transfers between devices: none -> 46.9 us  [the longest x7 25.5 us: divide_turns(): a_now = lax.ppermute(odd[-1], 'patch', pieces_in)]
    unnamed x24 -> x81, local copies, waits for them, and re-layouts: 2.04 us -> 17.1 us
    reduce_scatter x1, waiting for transfers between devices: 8.37 us -> 18.7 us  [local(): lax.psum_scatter(flux_sum, 'visit', scatter_dimension=0, tiled=True)]
  transfers between devices with their start and end apart: 7 -> 21, of which waited for: 5 -> 12; matrix products, arithmetic and copies ran while one was open for 0% -> 1% of each run, Pallas kernels for 0% -> 0%
where the time goes in v1:
time: 744 us; the launch traced here: 739 us
  loops' own time  185 us (25%)
  matrix products  141 us (19%)
  local copies, waits for them, and re-layouts  128 us (17%)
  starting transfers between devices  101 us (14%)
  waiting for transfers between devices  87 us (12%)
  other arithmetic  71.6 us (10%)
  between operations  26.1 us (4%)
    another operation x1, loops' own time, local(): flux_sum, cover_sum = lax.fori_loop(0, arrived.shape[0], visit_one, empty)  128 us
    dot_general x96, matrix products, match_exposure(): jnp.einsum('drw,xw->drx', smoothed[group, :count], col_band[group, x_degr...  108 us
    ppermute x7, starting transfers between devices, divide_turns(): a_now = lax.ppermute(odd[-1], 'patch', pieces_in)  78.1 us
    dynamic_slice x96, local copies, waits for them, and re-layouts, visit_one(): hit_second = table[offset, 1] == own_patch  62.7 us
    another operation x96, loops' own time, visit_one(): lax.cond(hit_first | hit_second, lambda: add_exposure(inner, exposure, of...  56 us
    dot_general x15, matrix products, warp_exposure(): warped = jnp.dot(middle, col_map, preferred_element_type=jnp.float32)  28.8 us
    ppermute x7, waiting for transfers between devices, divide_turns(): a_now = lax.ppermute(odd[-1], 'patch', pieces_in)  25.5 us
    ppermute x8, waiting for transfers between devices, divide_turns(): local_out = lax.ppermute(vec_out[-1], 'patch', line_up)  21.4 us
  transfers between devices with their start and end apart: 21, of which 12 were waited for; matrix products, arithmetic and copies ran while one was open for 1% of the time, Pallas kernels for 0%

profile of v1, /device:TPU:5, one launch (start us, length us, event | category | flops | bytes accessed | tf_op | source)
XLA Modules:
  0.0 739.3 jit_solution(8303537450106149658)
XLA Ops:
  51.2 119.2 %while.28 = (s32[]{:T(128)}, bf16[6,128,512]{2,1,0:T(8,128)(2,1)S(1)}, f32[6,3,40]{2,1,0:T(4,128)S(1)}, bf16[6,128,512]{1,2,0:T(8,128)(2,1)S(1)}, bf16[4,4,128,1...) while((s32[]{:T(128)}, ...), condition=%wide.region_53.54_spmd.clone.clone, body=%wide.region_16.53_spmd.clone.clone.sunk | while | flops 2971667456 | bytes 70542368 | solution.py:143
  52.3 2.0 multiply_reduce_fusion.58
  62.7 8.5 %fusion.219 = bf16[6,128,512]{2,1,0:T(8,128)(2,1)S(1)} fusion(bf16[6,128,512]{2,1,0:T(8,128)(2,1)S(1)} %get-tuple-element.857, s32[]{:T(128)} %get-tuple-element.856, bf16[4,4,512,512]{3,2,1,0:T(8,128)(2,1)S(1)} %copy-done, f32[128,512]{1,0:T(8,128)S(1)} %get-tuple-element.764, f32[128,512]{1,0:T(8,128)S(1)} %get-tuple-element.765, ...), kind=kOutput, calls=%fused_computation.133.clone.1 | convolution fusion | flops 73138176 | bytes 11012660 | tf_op jit(solution)/shard_map/while/body/eval_jaxpr/drw,xw->drx/dot_general | solution.py:72
  72.1 2.0 multiply_reduce_fusion.58
  82.5 8.5 %fusion.219 = bf16[6,128,512]{2,1,0:T(8,128)(2,1)S(1)} fusion(bf16[6,128,512]{2,1,0:T(8,128)(2,1)S(1)} %get-tuple-element.857, s32[]{:T(128)} %get-tuple-element.856, bf16[4,4,512,512]{3,2,1,0:T(8,128)(2,1)S(1)} %copy-done, f32[128,512]{1,0:T(8,128)S(1)} %get-tuple-element.764, f32[128,512]{1,0:T(8,128)S(1)} %get-tuple-element.765, ...), kind=kOutput, calls=%fused_computation.133.clone.1 | convolution fusion | flops 73138176 | bytes 11012660 | tf_op jit(solution)/shard_map/while/body/eval_jaxpr/drw,xw->drx/dot_general | solution.py:72
  91.9 2.0 multiply_reduce_fusion.58
  102.4 8.5 %fusion.219 = bf16[6,128,512]{2,1,0:T(8,128)(2,1)S(1)} fusion(bf16[6,128,512]{2,1,0:T(8,128)(2,1)S(1)} %get-tuple-element.857, s32[]{:T(128)} %get-tuple-element.856, bf16[4,4,512,512]{3,2,1,0:T(8,128)(2,1)S(1)} %copy-done, f32[128,512]{1,0:T(8,128)S(1)} %get-tuple-element.764, f32[128,512]{1,0:T(8,128)S(1)} %get-tuple-element.765, ...), kind=kOutput, calls=%fused_computation.133.clone.1 | convolution fusion | flops 73138176 | bytes 11012660 | tf_op jit(solution)/shard_map/while/body/eval_jaxpr/drw,xw->drx/dot_general | solution.py:72
  111.8 2.0 multiply_reduce_fusion.58
  122.2 8.5 %fusion.219 = bf16[6,128,512]{2,1,0:T(8,128)(2,1)S(1)} fusion(bf16[6,128,512]{2,1,0:T(8,128)(2,1)S(1)} %get-tuple-element.857, s32[]{:T(128)} %get-tuple-element.856, bf16[4,4,512,512]{3,2,1,0:T(8,128)(2,1)S(1)} %copy-done, f32[128,512]{1,0:T(8,128)S(1)} %get-tuple-element.764, f32[128,512]{1,0:T(8,128)S(1)} %get-tuple-element.765, ...), kind=kOutput, calls=%fused_computation.133.clone.1 | convolution fusion | flops 73138176 | bytes 11012660 | tf_op jit(solution)/shard_map/while/body/eval_jaxpr/drw,xw->drx/dot_general | solution.py:72
  131.6 2.0 multiply_reduce_fusion.58
  142.0 8.5 %fusion.219 = bf16[6,128,512]{2,1,0:T(8,128)(2,1)S(1)} fusion(bf16[6,128,512]{2,1,0:T(8,128)(2,1)S(1)} %get-tuple-element.857, s32[]{:T(128)} %get-tuple-element.856, bf16[4,4,512,512]{3,2,1,0:T(8,128)(2,1)S(1)} %copy-done, f32[128,512]{1,0:T(8,128)S(1)} %get-tuple-element.764, f32[128,512]{1,0:T(8,128)S(1)} %get-tuple-element.765, ...), kind=kOutput, calls=%fused_computation.133.clone.1 | convolution fusion | flops 73138176 | bytes 11012660 | tf_op jit(solution)/shard_map/while/body/eval_jaxpr/drw,xw->drx/dot_general | solution.py:72
  151.4 2.0 multiply_reduce_fusion.58
  161.9 8.5 %fusion.219 = bf16[6,128,512]{2,1,0:T(8,128)(2,1)S(1)} fusion(bf16[6,128,512]{2,1,0:T(8,128)(2,1)S(1)} %get-tuple-element.857, s32[]{:T(128)} %get-tuple-element.856, bf16[4,4,512,512]{3,2,1,0:T(8,128)(2,1)S(1)} %copy-done, f32[128,512]{1,0:T(8,128)S(1)} %get-tuple-element.764, f32[128,512]{1,0:T(8,128)S(1)} %get-tuple-element.765, ...), kind=kOutput, calls=%fused_computation.133.clone.1 | convolution fusion | flops 73138176 | bytes 11012660 | tf_op jit(solution)/shard_map/while/body/eval_jaxpr/drw,xw->drx/dot_general | solution.py:72
  172.3 8.9 %collective-permute-done = bf16[6,128,512]{2,1,0:T(8,128)(2,1)S(1)} collective-permute-done((bf16[6,128,512]{2,1,0:T(8,128)(2,1)S(1)}, bf16[6,128,512]{2,1,0:T(8,128)(2,1)S(1)}, u32[]{:S(2)}, u32[]{:S(2)}) %collective-permute-start) | collective-permute-done | bytes 786464 | tf_op jit(solution)/shard_map/ppermute | solution.py:21
  181.2 3.4 collective-permute-start.1
  184.6 9.0 %collective-permute-done.1 = bf16[6,128,512]{2,1,0:T(8,128)(2,1)S(1)} collective-permute-done((bf16[6,128,512]{2,1,0:T(8,128)(2,1)S(1)}, bf16[6,128,512]{2,1,0:T(8,128)(2,1)S(1)}, u32[]{:S(2)}, u32[]{:S(2)}) %collective-permute-start.1) | collective-permute-done | bytes 786464 | tf_op jit(solution)/shard_map/ppermute | solution.py:21
  193.6 3.4 collective-permute-start.2
  197.0 5.5 collective-permute-start.9
  202.5 3.5 collective-permute-done.2
  206.0 3.4 collective-permute-start.3
  209.4 3.0 collective-permute-done.9
  212.5 15.6 %collective-permute-start.10 = (bf16[6,128,512]{2,1,0:T(8,128)(2,1)S(1)}, bf16[6,128,512]{2,1,0:T(8,128)(2,1)S(1)}, u32[]{:S(2)}, u32[]{:S(2)}) collective-permute-start(bf16[6,128,512]{2,1,0:T(8,128)(2,1)S(1)} %collective-permute-done.9), channel_id=1, source_target_pairs={{0,15},{1,0},{2,1},{3,2},{4,3},{5,4},{6,5},{7,6},{8,7},{9,8},{10,9... | collective-permute-start | bytes 2359304 | tf_op jit(solution)/shard_map/ppermute | solution.py:24
  228.1 5.5 collective-permute-done.10
  233.6 14.3 %collective-permute-start.11 = (bf16[6,128,512]{2,1,0:T(8,128)(2,1)S(1)}, bf16[6,128,512]{2,1,0:T(8,128)(2,1)S(1)}, u32[]{:S(2)}, u32[]{:S(2)}) collective-permute-start(bf16[6,128,512]{2,1,0:T(8,128)(2,1)S(1)} %collective-permute-done.10), channel_id=1, source_target_pairs={{0,15},{1,0},{2,1},{3,2},{4,3},{5,4},{6,5},{7,6},{8,7},{9,8},{10,9... | collective-permute-start | bytes 2359304 | tf_op jit(solution)/shard_map/ppermute | solution.py:24
  248.0 5.5 collective-permute-done.11
  254.3 14.3 %collective-permute-start.12 = (bf16[6,128,512]{2,1,0:T(8,128)(2,1)S(1)}, bf16[6,128,512]{2,1,0:T(8,128)(2,1)}, u32[]{:S(2)}, u32[]{:S(2)}) collective-permute-start(bf16[6,128,512]{2,1,0:T(8,128)(2,1)S(1)} %collective-permute-done.11), channel_id=1, source_target_pairs={{0,15},{1,0},{2,1},{3,2},{4,3},{5,4},{6,5},{7,6},{8,7},{9,8},{10,9... | collective-permute-start | bytes 2359304 | tf_op jit(solution)/shard_map/ppermute | solution.py:24
  268.6 5.6 collective-permute-done.12
  274.3 14.2 %collective-permute-start.13 = (bf16[6,128,512]{2,1,0:T(8,128)(2,1)}, bf16[6,128,512]{2,1,0:T(8,128)(2,1)}, u32[]{:S(2)}, u32[]{:S(2)}) collective-permute-start(bf16[6,128,512]{2,1,0:T(8,128)(2,1)} %collective-permute-done.12), channel_id=1, source_target_pairs={{0,15},{1,0},{2,1},{3,2},{4,3},{5,4},{6,5},{7,6},{8,7},{9,8},{10,9... | collective-permute-start | bytes 2359304 | tf_op jit(solution)/shard_map/ppermute | solution.py:24
  288.6 5.8 collective-permute-done.13
  294.4 14.3 %collective-permute-start.14 = (bf16[6,128,512]{2,1,0:T(8,128)(2,1)}, bf16[6,128,512]{2,1,0:T(8,128)(2,1)S(1)}, u32[]{:S(2)}, u32[]{:S(2)}) collective-permute-start(bf16[6,128,512]{2,1,0:T(8,128)(2,1)} %collective-permute-done.13), channel_id=1, source_target_pairs={{0,15},{1,0},{2,1},{3,2},{4,3},{5,4},{6,5},{7,6},{8,7},{9,8},{10,9... | collective-permute-start | bytes 2359304 | tf_op jit(solution)/shard_map/ppermute | solution.py:24
  324.3 5.3 constant_dynamic-slice_fusion.4
  329.7 335.8 %while.27 = (s32[]{:T(128)}, f32[128,512]{1,0:T(8,128)S(1)}, f32[128,512]{1,0:T(8,128)S(1)}, s32[96,2]{0,1:T(2,128)S(1)}, s32[]{:T(128)}, /*index=5*/f32[96]{0:T...) while((s32[]{:T(128)}, f32[128,512]{1,0:T(8,128)S(1)}, ...), condition=%wide.region_59.60_spmd, body=%wide.region_54.59_spmd.sunk | while | flops 88949520 | bytes 1204658 | solution.py:173
  339.7 9.6 %conditional.2 = ((f32[128,512]{1,0:T(8,128)S(1)}, f32[128,512]{1,0:T(8,128)S(1)})) conditional(s32[]{:T(128)} %convert_element_type.1283, (f32[128,512]{1,0:T(8,128)S(1)}, f32[128,512]{1,0:T(8,128)S(1)}) %tuple.161, (s32[]{:T(128)}, f32[96]{0:T(128)S(1)}, s32[96]{0:T(128)S(1)}, f32[96,2]{0,1:T(2,128)S(1)}, bf16[96,128,512]{2,1,0:T(8,128)(2,1)}, ...), branch_computations={%region_55.55_spmd, %region_56.58_spmd} | conditional | flops 88949512 | bytes 1204415 | solution.py:167
  347.4 1.9 fusion.4
  375.2 9.6 %conditional.2 = ((f32[128,512]{1,0:T(8,128)S(1)}, f32[128,512]{1,0:T(8,128)S(1)})) conditional(s32[]{:T(128)} %convert_element_type.1283, (f32[128,512]{1,0:T(8,128)S(1)}, f32[128,512]{1,0:T(8,128)S(1)}) %tuple.161, (s32[]{:T(128)}, f32[96]{0:T(128)S(1)}, s32[96]{0:T(128)S(1)}, f32[96,2]{0,1:T(2,128)S(1)}, bf16[96,128,512]{2,1,0:T(8,128)(2,1)}, ...), branch_computations={%region_55.55_spmd, %region_56.58_spmd} | conditional | flops 88949512 | bytes 1204415 | solution.py:167
  382.9 1.9 fusion.4
  394.8 9.6 %conditional.2 = ((f32[128,512]{1,0:T(8,128)S(1)}, f32[128,512]{1,0:T(8,128)S(1)})) conditional(s32[]{:T(128)} %convert_element_type.1283, (f32[128,512]{1,0:T(8,128)S(1)}, f32[128,512]{1,0:T(8,128)S(1)}) %tuple.161, (s32[]{:T(128)}, f32[96]{0:T(128)S(1)}, s32[96]{0:T(128)S(1)}, f32[96,2]{0,1:T(2,128)S(1)}, bf16[96,128,512]{2,1,0:T(8,128)(2,1)}, ...), branch_computations={%region_55.55_spmd, %region_56.58_spmd} | conditional | flops 88949512 | bytes 1204415 | solution.py:167
  402.5 1.9 fusion.4
  414.4 9.6 %conditional.2 = ((f32[128,512]{1,0:T(8,128)S(1)}, f32[128,512]{1,0:T(8,128)S(1)})) conditional(s32[]{:T(128)} %convert_element_type.1283, (f32[128,512]{1,0:T(8,128)S(1)}, f32[128,512]{1,0:T(8,128)S(1)}) %tuple.161, (s32[]{:T(128)}, f32[96]{0:T(128)S(1)}, s32[96]{0:T(128)S(1)}, f32[96,2]{0,1:T(2,128)S(1)}, bf16[96,128,512]{2,1,0:T(8,128)(2,1)}, ...), branch_computations={%region_55.55_spmd, %region_56.58_spmd} | conditional | flops 88949512 | bytes 1204415 | solution.py:167
  422.1 1.9 fusion.4
  434.0 9.6 %conditional.2 = ((f32[128,512]{1,0:T(8,128)S(1)}, f32[128,512]{1,0:T(8,128)S(1)})) conditional(s32[]{:T(128)} %convert_element_type.1283, (f32[128,512]{1,0:T(8,128)S(1)}, f32[128,512]{1,0:T(8,128)S(1)}) %tuple.161, (s32[]{:T(128)}, f32[96]{0:T(128)S(1)}, s32[96]{0:T(128)S(1)}, f32[96,2]{0,1:T(2,128)S(1)}, bf16[96,128,512]{2,1,0:T(8,128)(2,1)}, ...), branch_computations={%region_55.55_spmd, %region_56.58_spmd} | conditional | flops 88949512 | bytes 1204415 | solution.py:167
  441.7 1.9 fusion.4
  451.6 9.6 %conditional.2 = ((f32[128,512]{1,0:T(8,128)S(1)}, f32[128,512]{1,0:T(8,128)S(1)})) conditional(s32[]{:T(128)} %convert_element_type.1283, (f32[128,512]{1,0:T(8,128)S(1)}, f32[128,512]{1,0:T(8,128)S(1)}) %tuple.161, (s32[]{:T(128)}, f32[96]{0:T(128)S(1)}, s32[96]{0:T(128)S(1)}, f32[96,2]{0,1:T(2,128)S(1)}, bf16[96,128,512]{2,1,0:T(8,128)(2,1)}, ...), branch_computations={%region_55.55_spmd, %region_56.58_spmd} | conditional | flops 88949512 | bytes 1204415 | solution.py:167
  459.3 1.9 fusion.4
  473.2 9.6 %conditional.2 = ((f32[128,512]{1,0:T(8,128)S(1)}, f32[128,512]{1,0:T(8,128)S(1)})) conditional(s32[]{:T(128)} %convert_element_type.1283, (f32[128,512]{1,0:T(8,128)S(1)}, f32[128,512]{1,0:T(8,128)S(1)}) %tuple.161, (s32[]{:T(128)}, f32[96]{0:T(128)S(1)}, s32[96]{0:T(128)S(1)}, f32[96,2]{0,1:T(2,128)S(1)}, bf16[96,128,512]{2,1,0:T(8,128)(2,1)}, ...), branch_computations={%region_55.55_spmd, %region_56.58_spmd} | conditional | flops 88949512 | bytes 1204415 | solution.py:167
  480.9 1.9 fusion.4
  494.8 9.6 %conditional.2 = ((f32[128,512]{1,0:T(8,128)S(1)}, f32[128,512]{1,0:T(8,128)S(1)})) conditional(s32[]{:T(128)} %convert_element_type.1283, (f32[128,512]{1,0:T(8,128)S(1)}, f32[128,512]{1,0:T(8,128)S(1)}) %tuple.161, (s32[]{:T(128)}, f32[96]{0:T(128)S(1)}, s32[96]{0:T(128)S(1)}, f32[96,2]{0,1:T(2,128)S(1)}, bf16[96,128,512]{2,1,0:T(8,128)(2,1)}, ...), branch_computations={%region_55.55_spmd, %region_56.58_spmd} | conditional | flops 88949512 | bytes 1204415 | solution.py:167
  522.4 9.6 %conditional.2 = ((f32[128,512]{1,0:T(8,128)S(1)}, f32[128,512]{1,0:T(8,128)S(1)})) conditional(s32[]{:T(128)} %convert_element_type.1283, (f32[128,512]{1,0:T(8,128)S(1)}, f32[128,512]{1,0:T(8,128)S(1)}) %tuple.161, (s32[]{:T(128)}, f32[96]{0:T(128)S(1)}, s32[96]{0:T(128)S(1)}, f32[96,2]{0,1:T(2,128)S(1)}, bf16[96,128,512]{2,1,0:T(8,128)(2,1)}, ...), branch_computations={%region_55.55_spmd, %region_56.58_spmd} | conditional | flops 88949512 | bytes 1204415 | solution.py:167
  530.1 1.9 fusion.4
  543.9 9.6 %conditional.2 = ((f32[128,512]{1,0:T(8,128)S(1)}, f32[128,512]{1,0:T(8,128)S(1)})) conditional(s32[]{:T(128)} %convert_element_type.1283, (f32[128,512]{1,0:T(8,128)S(1)}, f32[128,512]{1,0:T(8,128)S(1)}) %tuple.161, (s32[]{:T(128)}, f32[96]{0:T(128)S(1)}, s32[96]{0:T(128)S(1)}, f32[96,2]{0,1:T(2,128)S(1)}, bf16[96,128,512]{2,1,0:T(8,128)(2,1)}, ...), branch_computations={%region_55.55_spmd, %region_56.58_spmd} | conditional | flops 88949512 | bytes 1204415 | solution.py:167
  569.5 9.6 %conditional.2 = ((f32[128,512]{1,0:T(8,128)S(1)}, f32[128,512]{1,0:T(8,128)S(1)})) conditional(s32[]{:T(128)} %convert_element_type.1283, (f32[128,512]{1,0:T(8,128)S(1)}, f32[128,512]{1,0:T(8,128)S(1)}) %tuple.161, (s32[]{:T(128)}, f32[96]{0:T(128)S(1)}, s32[96]{0:T(128)S(1)}, f32[96,2]{0,1:T(2,128)S(1)}, bf16[96,128,512]{2,1,0:T(8,128)(2,1)}, ...), branch_computations={%region_55.55_spmd, %region_56.58_spmd} | conditional | flops 88949512 | bytes 1204415 | solution.py:167
  585.1 9.6 %conditional.2 = ((f32[128,512]{1,0:T(8,128)S(1)}, f32[128,512]{1,0:T(8,128)S(1)})) conditional(s32[]{:T(128)} %convert_element_type.1283, (f32[128,512]{1,0:T(8,128)S(1)}, f32[128,512]{1,0:T(8,128)S(1)}) %tuple.161, (s32[]{:T(128)}, f32[96]{0:T(128)S(1)}, s32[96]{0:T(128)S(1)}, f32[96,2]{0,1:T(2,128)S(1)}, bf16[96,128,512]{2,1,0:T(8,128)(2,1)}, ...), branch_computations={%region_55.55_spmd, %region_56.58_spmd} | conditional | flops 88949512 | bytes 1204415 | solution.py:167
  610.7 9.6 %conditional.2 = ((f32[128,512]{1,0:T(8,128)S(1)}, f32[128,512]{1,0:T(8,128)S(1)})) conditional(s32[]{:T(128)} %convert_element_type.1283, (f32[128,512]{1,0:T(8,128)S(1)}, f32[128,512]{1,0:T(8,128)S(1)}) %tuple.161, (s32[]{:T(128)}, f32[96]{0:T(128)S(1)}, s32[96]{0:T(128)S(1)}, f32[96,2]{0,1:T(2,128)S(1)}, bf16[96,128,512]{2,1,0:T(8,128)(2,1)}, ...), branch_computations={%region_55.55_spmd, %region_56.58_spmd} | conditional | flops 88949512 | bytes 1204415 | solution.py:167
  626.3 9.6 %conditional.2 = ((f32[128,512]{1,0:T(8,128)S(1)}, f32[128,512]{1,0:T(8,128)S(1)})) conditional(s32[]{:T(128)} %convert_element_type.1283, (f32[128,512]{1,0:T(8,128)S(1)}, f32[128,512]{1,0:T(8,128)S(1)}) %tuple.161, (s32[]{:T(128)}, f32[96]{0:T(128)S(1)}, s32[96]{0:T(128)S(1)}, f32[96,2]{0,1:T(2,128)S(1)}, bf16[96,128,512]{2,1,0:T(8,128)(2,1)}, ...), branch_computations={%region_55.55_spmd, %region_56.58_spmd} | conditional | flops 88949512 | bytes 1204415 | solution.py:167
  651.9 9.6 %conditional.2 = ((f32[128,512]{1,0:T(8,128)S(1)}, f32[128,512]{1,0:T(8,128)S(1)})) conditional(s32[]{:T(128)} %convert_element_type.1283, (f32[128,512]{1,0:T(8,128)S(1)}, f32[128,512]{1,0:T(8,128)S(1)}) %tuple.161, (s32[]{:T(128)}, f32[96]{0:T(128)S(1)}, s32[96]{0:T(128)S(1)}, f32[96,2]{0,1:T(2,128)S(1)}, bf16[96,128,512]{2,1,0:T(8,128)(2,1)}, ...), branch_computations={%region_55.55_spmd, %region_56.58_spmd} | conditional | flops 88949512 | bytes 1204415 | solution.py:167
  668.3 18.7 %reduce-scatter.3.cloned.1.call-done = f32[64,512]{1,0:T(8,128)} async-done(((f32[128,512]{1,0:T(8,128)}), f32[64,512]{1,0:T(8,128)}) %reduce-scatter.3.cloned.1.call-update) | async-done | bytes 131088 | tf_op jit(solution)/shard_map/reduce_scatter | solution.py:175
  687.0 14.0 %reduce-scatter.5.cloned.1.call-done = f32[64,512]{1,0:T(8,128)} async-done(((f32[128,512]{1,0:T(8,128)}), f32[64,512]{1,0:T(8,128)}) %reduce-scatter.5.cloned.1.call-update) | async-done | bytes 131088 | tf_op jit(solution)/shard_map/reduce_scatter | solution.py:176
  702.0 2.2 collective-permute-start.15
  705.5 3.1 collective-permute-done.16
  708.7 5.2 collective-permute-start.17
  713.9 1.9 collective-permute-start.18
  716.5 3.6 collective-permute-done.18
  720.2 5.7 fusion.128
  725.9 6.5 fusion.136
  (638 shorter events, 248.9 us)
Async XLA Ops:
  7.2 43.7 %copy-start.18 = (bf16[1,6,128,512]{3,2,1,0:T(8,128)(2,1)S(1)}, bf16[1,6,128,512]{3,2,1,0:T(8,128)(2,1)}, u32[]{:S(2)}) copy-start(bf16[1,6,128,512]{3,2,1,0:T(8,128)(2,1)} %param.13) | copy-start | bytes 2359300
  7.2 44.1 %copy-start.21 = (f32[1,6,3,40]{3,0,2,1:T(1,128)S(1)}, f32[1,6,3,40]{3,0,2,1:T(1,128)}, u32[]{:S(2)}) copy-start(f32[1,6,3,40]{3,0,2,1:T(1,128)} %param.14) | copy-start | bytes 8644
  7.2 679.8 %reduce-scatter.3.cloned.1.call-start = ((), (), s32[]{:S(2)}) async-start(), calls=%async_computation.2 | async-start | bytes 393216 | tf_op jit(solution)/shard_map/reduce_scatter | solution.py:175
  51.4 4.7 copy-start
  71.3 4.7 copy-start
  91.1 4.7 copy-start
  110.9 4.7 copy-start
  130.8 4.7 copy-start
  150.6 4.7 copy-start
  170.4 26.6 %copy-start.12 = (bf16[6,128,512]{2,1,0:T(8,128)(2,1)}, bf16[6,128,512]{2,1,0:T(8,128)(2,1)S(1)}, u32[]{:S(2)}) copy-start(bf16[6,128,512]{2,1,0:T(8,128)(2,1)S(1)} %get-tuple-element.365) | copy-start | bytes 2359300
  170.4 10.8 %collective-permute-start = (bf16[6,128,512]{2,1,0:T(8,128)(2,1)S(1)}, bf16[6,128,512]{2,1,0:T(8,128)(2,1)S(1)}, u32[]{:S(2)}, u32[]{:S(2)}) collective-permute-start(bf16[6,128,512]{2,1,0:T(8,128)(2,1)S(1)} %get-tuple-element.365), channel_id=1, source_target_pairs={{0,1},{1,2},{2,3},{3,4},{4,5},{5,6},{6,7},{7,8},{8,9},{9,10},{10,1... | collective-permute-start | bytes 2359304 | tf_op jit(solution)/shard_map/ppermute | solution.py:21
  181.2 12.4 %collective-permute-start.1 = (bf16[6,128,512]{2,1,0:T(8,128)(2,1)S(1)}, bf16[6,128,512]{2,1,0:T(8,128)(2,1)S(1)}, u32[]{:S(2)}, u32[]{:S(2)}) collective-permute-start(bf16[6,128,512]{2,1,0:T(8,128)(2,1)S(1)} %collective-permute-done), channel_id=1, source_target_pairs={{0,1},{1,2},{2,3},{3,4},{4,5},{5,6},{6,7},{7,8},{8,9},{9,10},{10,1... | collective-permute-start | bytes 2359304 | tf_op jit(solution)/shard_map/ppermute | solution.py:21
  184.6 12.4 %collective-permute-start.8 = (bf16[6,128,512]{2,1,0:T(8,128)(2,1)S(1)}, bf16[6,128,512]{2,1,0:T(8,128)(2,1)S(1)}, u32[]{:S(2)}, u32[]{:S(2)}) collective-permute-start(bf16[6,128,512]{2,1,0:T(8,128)(2,1)S(1)} %get-tuple-element.365), channel_id=1, source_target_pairs={{0,15},{1,0},{2,1},{3,2},{4,3},{5,4},{6,5},{7,6},{8,7},{9,8},{10,9... | collective-permute-start | bytes 2359304 | tf_op jit(solution)/shard_map/ppermute | solution.py:24
  193.6 12.4 %collective-permute-start.2 = (bf16[6,128,512]{2,1,0:T(8,128)(2,1)S(1)}, bf16[6,128,512]{2,1,0:T(8,128)(2,1)S(1)}, u32[]{:S(2)}, u32[]{:S(2)}) collective-permute-start(bf16[6,128,512]{2,1,0:T(8,128)(2,1)S(1)} %collective-permute-done.1), channel_id=1, source_target_pairs={{0,1},{1,2},{2,3},{3,4},{4,5},{5,6},{6,7},{7,8},{8,9},{9,10},{10,1... | collective-permute-start | bytes 2359304 | tf_op jit(solution)/shard_map/ppermute | solution.py:21
  197.0 15.4 %collective-permute-start.9 = (bf16[6,128,512]{2,1,0:T(8,128)(2,1)S(1)}, bf16[6,128,512]{2,1,0:T(8,128)(2,1)S(1)}, u32[]{:S(2)}, u32[]{:S(2)}) collective-permute-start(bf16[6,128,512]{2,1,0:T(8,128)(2,1)S(1)} %collective-permute-done.8), channel_id=1, source_target_pairs={{0,15},{1,0},{2,1},{3,2},{4,3},{5,4},{6,5},{7,6},{8,7},{9,8},{10,9... | collective-permute-start | bytes 2359304 | tf_op jit(solution)/shard_map/ppermute | solution.py:24
  206.0 27.6 %copy-start.2 = (bf16[6,128,512]{2,1,0:T(8,128)(2,1)}, bf16[6,128,512]{2,1,0:T(8,128)(2,1)S(1)}, u32[]{:S(2)}) copy-start(bf16[6,128,512]{2,1,0:T(8,128)(2,1)S(1)} %collective-permute-done.2) | copy-start | bytes 2359300
  206.0 22.0 %collective-permute-start.3 = (bf16[6,128,512]{2,1,0:T(8,128)(2,1)S(1)}, bf16[6,128,512]{2,1,0:T(8,128)(2,1)S(1)}, u32[]{:S(2)}, u32[]{:S(2)}) collective-permute-start(bf16[6,128,512]{2,1,0:T(8,128)(2,1)S(1)} %collective-permute-done.2), channel_id=1, source_target_pairs={{0,1},{1,2},{2,3},{3,4},{4,5},{5,6},{6,7},{7,8},{8,9},{9,10},{10,1... | collective-permute-start | bytes 2359304 | tf_op jit(solution)/shard_map/ppermute | solution.py:21
  212.5 21.1 %collective-permute-start.10 = (bf16[6,128,512]{2,1,0:T(8,128)(2,1)S(1)}, bf16[6,128,512]{2,1,0:T(8,128)(2,1)S(1)}, u32[]{:S(2)}, u32[]{:S(2)}) collective-permute-start(bf16[6,128,512]{2,1,0:T(8,128)(2,1)S(1)} %collective-permute-done.9), channel_id=1, source_target_pairs={{0,15},{1,0},{2,1},{3,2},{4,3},{5,4},{6,5},{7,6},{8,7},{9,8},{10,9... | collective-permute-start | bytes 2359304 | tf_op jit(solution)/shard_map/ppermute | solution.py:24
  228.0 46.2 %copy-start.8 = (bf16[6,128,512]{2,1,0:T(8,128)(2,1)}, bf16[6,128,512]{2,1,0:T(8,128)(2,1)S(1)}, u32[]{:S(2)}) copy-start(bf16[6,128,512]{2,1,0:T(8,128)(2,1)S(1)} %collective-permute-done.3) | copy-start | bytes 2359300
  228.0 19.8 %collective-permute-start.4 = (bf16[6,128,512]{2,1,0:T(8,128)(2,1)S(1)}, bf16[6,128,512]{2,1,0:T(8,128)(2,1)S(1)}, u32[]{:S(2)}, u32[]{:S(2)}) collective-permute-start(bf16[6,128,512]{2,1,0:T(8,128)(2,1)S(1)} %collective-permute-done.3), channel_id=1, source_target_pairs={{0,1},{1,2},{2,3},{3,4},{4,5},{5,6},{6,7},{7,8},{8,9},{9,10},{10,1... | collective-permute-start | bytes 2359304 | tf_op jit(solution)/shard_map/ppermute | solution.py:21
  233.6 14.3 %copy-start.4 = (bf16[6,128,512]{2,1,0:T(8,128)(2,1)}, bf16[6,128,512]{2,1,0:T(8,128)(2,1)S(1)}, u32[]{:S(2)}) copy-start(bf16[6,128,512]{2,1,0:T(8,128)(2,1)S(1)} %collective-permute-done.10) | copy-start | bytes 2359300
  233.6 19.8 %collective-permute-start.11 = (bf16[6,128,512]{2,1,0:T(8,128)(2,1)S(1)}, bf16[6,128,512]{2,1,0:T(8,128)(2,1)S(1)}, u32[]{:S(2)}, u32[]{:S(2)}) collective-permute-start(bf16[6,128,512]{2,1,0:T(8,128)(2,1)S(1)} %collective-permute-done.10), channel_id=1, source_target_pairs={{0,15},{1,0},{2,1},{3,2},{4,3},{5,4},{6,5},{7,6},{8,7},{9,8},{10,9... | collective-permute-start | bytes 2359304 | tf_op jit(solution)/shard_map/ppermute | solution.py:24
  247.9 40.6 %copy-start.10 = (bf16[6,128,512]{2,1,0:T(8,128)(2,1)}, bf16[6,128,512]{2,1,0:T(8,128)(2,1)S(1)}, u32[]{:S(2)}) copy-start(bf16[6,128,512]{2,1,0:T(8,128)(2,1)S(1)} %collective-permute-done.4) | copy-start | bytes 2359300
  247.9 20.7 %collective-permute-start.5 = (bf16[6,128,512]{2,1,0:T(8,128)(2,1)S(1)}, bf16[6,128,512]{2,1,0:T(8,128)(2,1)S(1)}, u32[]{:S(2)}, u32[]{:S(2)}) collective-permute-start(bf16[6,128,512]{2,1,0:T(8,128)(2,1)S(1)} %collective-permute-done.4), channel_id=1, source_target_pairs={{0,1},{1,2},{2,3},{3,4},{4,5},{5,6},{6,7},{7,8},{8,9},{9,10},{10,1... | collective-permute-start | bytes 2359304 | tf_op jit(solution)/shard_map/ppermute | solution.py:21
  253.4 0.9 copy-start.6
  254.3 19.9 %collective-permute-start.12 = (bf16[6,128,512]{2,1,0:T(8,128)(2,1)S(1)}, bf16[6,128,512]{2,1,0:T(8,128)(2,1)}, u32[]{:S(2)}, u32[]{:S(2)}) collective-permute-start(bf16[6,128,512]{2,1,0:T(8,128)(2,1)S(1)} %collective-permute-done.11), channel_id=1, source_target_pairs={{0,15},{1,0},{2,1},{3,2},{4,3},{5,4},{6,5},{7,6},{8,7},{9,8},{10,9... | collective-permute-start | bytes 2359304 | tf_op jit(solution)/shard_map/ppermute | solution.py:24
  268.6 19.9 %copy-start.14 = (bf16[6,128,512]{2,1,0:T(8,128)(2,1)}, bf16[6,128,512]{2,1,0:T(8,128)(2,1)S(1)}, u32[]{:S(2)}) copy-start(bf16[6,128,512]{2,1,0:T(8,128)(2,1)S(1)} %collective-permute-done.5) | copy-start | bytes 2359300
  268.6 19.8 %collective-permute-start.6 = (bf16[6,128,512]{2,1,0:T(8,128)(2,1)S(1)}, bf16[6,128,512]{2,1,0:T(8,128)(2,1)}, u32[]{:S(2)}, u32[]{:S(2)}) collective-permute-start(bf16[6,128,512]{2,1,0:T(8,128)(2,1)S(1)} %collective-permute-done.5), channel_id=1, source_target_pairs={{0,1},{1,2},{2,3},{3,4},{4,5},{5,6},{6,7},{7,8},{8,9},{9,10},{10,1... | collective-permute-start | bytes 2359304 | tf_op jit(solution)/shard_map/ppermute | solution.py:21
  274.3 20.2 %collective-permute-start.13 = (bf16[6,128,512]{2,1,0:T(8,128)(2,1)}, bf16[6,128,512]{2,1,0:T(8,128)(2,1)}, u32[]{:S(2)}, u32[]{:S(2)}) collective-permute-start(bf16[6,128,512]{2,1,0:T(8,128)(2,1)} %collective-permute-done.12), channel_id=1, source_target_pairs={{0,15},{1,0},{2,1},{3,2},{4,3},{5,4},{6,5},{7,6},{8,7},{9,8},{10,9... | collective-permute-start | bytes 2359304 | tf_op jit(solution)/shard_map/ppermute | solution.py:24
  288.5 20.3 %collective-permute-start.7 = (bf16[6,128,512]{2,1,0:T(8,128)(2,1)}, bf16[6,128,512]{2,1,0:T(8,128)(2,1)}, u32[]{:S(2)}, u32[]{:S(2)}) collective-permute-start(bf16[6,128,512]{2,1,0:T(8,128)(2,1)} %collective-permute-done.6), channel_id=1, source_target_pairs={{0,1},{1,2},{2,3},{3,4},{4,5},{5,6},{6,7},{7,8},{8,9},{9,10},{10,1... | collective-permute-start | bytes 2359304 | tf_op jit(solution)/shard_map/ppermute | solution.py:21
  288.6 26.3 %copy-start.3 = (bf16[6,128,512]{2,1,0:T(8,128)(2,1)S(1)}, bf16[6,128,512]{2,1,0:T(8,128)(2,1)}, u32[]{:S(2)}) copy-start(bf16[6,128,512]{2,1,0:T(8,128)(2,1)} %copy-done.2) | copy-start | bytes 2359300
  288.6 26.6 %copy-start.13 = (bf16[6,128,512]{2,1,0:T(8,128)(2,1)S(1)}, bf16[6,128,512]{2,1,0:T(8,128)(2,1)}, u32[]{:S(2)}) copy-start(bf16[6,128,512]{2,1,0:T(8,128)(2,1)} %copy-done.12) | copy-start | bytes 2359300
  288.6 26.9 %copy-start.5 = (bf16[6,128,512]{2,1,0:T(8,128)(2,1)S(1)}, bf16[6,128,512]{2,1,0:T(8,128)(2,1)}, u32[]{:S(2)}) copy-start(bf16[6,128,512]{2,1,0:T(8,128)(2,1)} %copy-done.4) | copy-start | bytes 2359300
  294.4 23.8 %collective-permute-start.14 = (bf16[6,128,512]{2,1,0:T(8,128)(2,1)}, bf16[6,128,512]{2,1,0:T(8,128)(2,1)S(1)}, u32[]{:S(2)}, u32[]{:S(2)}) collective-permute-start(bf16[6,128,512]{2,1,0:T(8,128)(2,1)} %collective-permute-done.13), channel_id=1, source_target_pairs={{0,15},{1,0},{2,1},{3,2},{4,3},{5,4},{6,5},{7,6},{8,7},{9,8},{10,9... | collective-permute-start | bytes 2359304 | tf_op jit(solution)/shard_map/ppermute | solution.py:24
  309.9 5.6 copy-start.7
  315.1 5.7 copy-start.15
  315.2 5.7 copy-start.11
  315.3 5.7 copy-start.9
  324.2 5.4 copy-start.19
  324.2 5.4 copy-start.20
  324.3 5.4 copy-start.22
  324.3 5.4 copy-start.23
  324.3 5.4 copy-start.24
  665.5 0.7 copy-start.17
  665.5 0.8 copy-start.1
  666.2 34.7 %reduce-scatter.5.cloned.1.call-start = ((), (), s32[]{:S(2)}) async-start(), calls=%async_computation.3 | async-start | bytes 393216 | tf_op jit(solution)/shard_map/reduce_scatter | solution.py:176
  702.0 30.5 %copy-start.16 = (f32[64,512]{1,0:T(8,128)}, f32[64,512]{1,0:T(8,128)S(1)}, u32[]{:S(2)}) copy-start(f32[64,512]{1,0:T(8,128)S(1)} %maximum_divide_fusion) | copy-start | bytes 393220
  702.0 3.5 collective-permute-start.15
  704.2 4.4 collective-permute-start.16
  708.7 7.9 %collective-permute-start.17 = (f32[72,4]{1,0:T(8,128)S(1)}, f32[72,4]{1,0:T(8,128)S(1)}, u32[]{:S(2)}, u32[]{:S(2)}) collective-permute-start(f32[72,4]{1,0:T(8,128)S(1)} %get-tuple-element.558), channel_id=1, source_target_pairs={{0,1},{1,2},{2,3},{3,4},{4,5},{5,6},{6,7},{7,8},{8,9},{9,10},{10,1... | collective-permute-start | bytes 3464 | tf_op jit(solution)/shard_map/ppermute | solution.py:38
  713.9 6.2 collective-permute-start.18
Sparse Core Ops, SparseCore 0:
  666.3 20.5 reduce-scatter.2
  689.2 11.7 reduce-scatter.4
